TPU v7x, 32 devices: a whole 2x2x4 slice. The times are simulated.
32 devices in a mesh: groups: 2 (over x), pts: 16 (over z, y, core).
Axes of the slice: x: 2, y: 2, z: 4, core: 2. Of those that a mesh axis runs over, the one named last changes fastest.
Arguments:
- points: bfloat16 [8192, 512], P(('groups', 'pts')), parts along dimension 0, may hold values from -6 to 6
- labels: int32 [8192], P(('groups', 'pts')), parts along dimension 0, may hold values from 0 to 15
- centres: bfloat16 [32768, 512], P(('groups', 'pts')), parts along dimension 0, may hold values from -6 to 6
- tri_inverse: bfloat16 [32768, 16384], P(('groups', 'pts')), parts along dimension 0, as said below
- beta: bfloat16 [32768, 16], P(('groups', 'pts')), parts along dimension 0, may hold values from -0.01171875 to 0.01171875
- bias: float32 [32], P('groups'), parts along dimension 0, may hold values from -3.2 to -2.2
Outputs:
- gradient: float32 [32768, 16], P(('groups', 'pts')), parts along dimension 0
- logits: float32 [8192, 16], P(('groups', 'pts')), parts along dimension 0
There are 2 independent parts, one for each index of `groups`. A program takes and returns all parts, laid end to end along the dimension named above; each array names one. Nothing has to cross between parts.
Inputs may be any that keep to these rules, and one draw needn't show every extreme that they name: `tri_inverse`: upper triangular: entries below the diagonal are zero; the diagonal lies between 0.6 and 1.4.
All inputs are finite; a program needn't handle non-finite values.
Results may differ from a plain program's by a relative error of at most 0.0039.
Values may be sent and summed in bfloat16 or wider, within the bound.
A program may use at most 128 MiB of HBM per device.

v0:
```python
import math
import jax
import jax.numpy as jnp
from jax import lax
from jax.sharding import PartitionSpec as P


def cube_kernel(point_block, centre_block):
    inner = lax.dot_general(
        point_block, centre_block, (((1,), (1,)), ((), ())), preferred_element_type=jnp.float32
    )
    factor = 1.0 / math.sqrt(point_block.shape[1])
    return ((inner * factor + 1.0) ** 3).astype(jnp.bfloat16)


def on_device(points, labels, centres, tri_inverse, beta, bias):
    local_points = points.shape[0]
    local_centres = centres.shape[0]
    class_count = beta.shape[1]
    packing = 128 // class_count
    dense_centres = local_centres // packing
    total_points = local_points * lax.axis_size("pts")
    beta_dense = beta.reshape(dense_centres, 128)
    beta_part = lax.all_gather(beta_dense, "pts", axis=0, tiled=True)
    narrow = beta_part.reshape(beta_part.shape[0] * packing, class_count)
    columns = tri_inverse
    alpha_sum = jnp.dot(columns, narrow, preferred_element_type=jnp.float32)
    alpha_local = alpha_sum.astype(jnp.bfloat16)
    alpha_dense = alpha_local.reshape(dense_centres, 128)
    classes_row = jnp.arange(class_count, dtype=jnp.int32)
    onehot = (labels[:, None] == classes_row[None, :]).astype(jnp.float32)
    parts_in = (
        lax.all_gather(centres, "pts", axis=0, tiled=True),
        lax.all_gather(alpha_dense, "pts", axis=0, tiled=True),
    )
    kernel_tile = cube_kernel(points, parts_in[0])
    narrow = parts_in[1].reshape(parts_in[1].shape[0] * packing, class_count)
    logit_sum = jnp.dot(kernel_tile, narrow, preferred_element_type=jnp.float32)
    logits = logit_sum + bias[None, :]
    resid = (jax.nn.sigmoid(logits) - onehot).astype(jnp.bfloat16)
    resid_dense = resid.reshape(local_points // packing, 128)
    parts_in = (
        lax.all_gather(points, "pts", axis=0, tiled=True),
        lax.all_gather(resid_dense, "pts", axis=0, tiled=True),
    )
    kernel_tile = cube_kernel(parts_in[0], centres)
    narrow = parts_in[1].reshape(parts_in[1].shape[0] * packing, class_count)
    grad_sum = lax.dot_general(
        kernel_tile, narrow, (((0,), (0,)), ((), ())), preferred_element_type=jnp.float32
    )
    grad_dense = grad_sum.reshape(dense_centres, 128)
    grad_kernel = (
        grad_dense.reshape(local_centres, class_count) * (1.0 / math.sqrt(total_points))
    ).astype(jnp.bfloat16)
    columns = tri_inverse
    term = lax.dot_general(
        columns, grad_kernel, (((0,), (0,)), ((), ())), preferred_element_type=jnp.float32
    )
    gradient_dense = lax.psum_scatter(
        term.reshape(lax.axis_size("pts") * dense_centres, 128),
        "pts",
        scatter_dimension=0,
        tiled=True,
    )
    return (gradient_dense.reshape(local_centres, class_count), logits)


def solution(mesh):
    return jax.shard_map(
        on_device,
        mesh=mesh,
        in_specs=(
            P(("groups", "pts"), None),
            P(("groups", "pts")),
            P(("groups", "pts"), None),
            P(("groups", "pts"), None),
            P(("groups", "pts"), None),
            P("groups"),
        ),
        out_specs=(P(("groups", "pts"), None), P(("groups", "pts"), None)),
        check_vma=False,
    )
```

profile of v0, /device:TPU:0, one launch (start us, length us, event | category | flops | bytes accessed | tf_op | source)
XLA Modules:
  0.0 295.3 jit_solution(16298011855423108095)
XLA Ops:
  7.2 0.7 all-gather.5.cloned.1.call-update
  7.9 0.7 all-gather.3.cloned.1.call-update
  8.7 0.9 copy.8
  9.6 0.2 reshape.30
  9.8 26.4 %all_gather.17 = bf16[2048,128]{1,0:T(8,128)(2,1)S(1)} all-gather(bf16[128,128]{1,0:T(8,128)(2,1)S(1)} %reshape.30), channel_id=1, replica_groups=mesh['groups'=2,'pts'=16] {'pts'}, dimensions={0}, use_global_device_ids=true | all-gather | bytes 557056 | tf_op jit(solution)/shard_map/all_gather | solution.py:24
  36.3 4.0 %reshape.31 = bf16[16384,16]{1,0:T(8,128)(2,1)} reshape(bf16[2048,128]{1,0:T(8,128)(2,1)S(1)} %all_gather.17) | data formatting | bytes 1048576 | tf_op jit(solution)/shard_map/reshape | solution.py:25
  40.3 15.4 %convolution_convert_fusion = bf16[1024,16]{0,1:T(8,128)(2,1)S(1)} fusion(bf16[1024,16384]{1,0:T(8,128)(2,1)} %param.9, bf16[16384,16]{1,0:T(8,128)(2,1)} %reshape.31), kind=kOutput, calls=%fused_computation.11 | convolution fusion | flops 536887296 | bytes 34111488 | tf_op jit(solution)/shard_map/dot_general | solution.py:27
  55.7 0.2 copy.9
  55.9 0.2 reshape.32
  56.0 20.5 %all_gather.18 = bf16[2048,128]{1,0:T(8,128)(2,1)S(1)} all-gather(bf16[128,128]{1,0:T(8,128)(2,1)S(1)} %reshape.32), channel_id=1, replica_groups=mesh['groups'=2,'pts'=16] {'pts'}, dimensions={0}, use_global_device_ids=true | all-gather | bytes 557056 | tf_op jit(solution)/shard_map/all_gather | solution.py:34
  76.5 4.0 %reshape.33 = bf16[16384,16]{1,0:T(8,128)(2,1)} reshape(bf16[2048,128]{1,0:T(8,128)(2,1)S(1)} %all_gather.18) | data formatting | bytes 1048576 | tf_op jit(solution)/shard_map/reshape | solution.py:37
  80.5 61.5 %all-gather.5.cloned.1.call-done = bf16[16384,512]{1,0:T(8,128)(2,1)} async-done(((bf16[1024,512]{1,0:T(8,128)(2,1)}), bf16[16384,512]{1,0:T(8,128)(2,1)}) %all-gather.5.cloned.1.call-update) | async-done | bytes 16777232 | tf_op jit(solution)/shard_map/all_gather | solution.py:33
  142.0 11.7 %subtract_convert_fusion = (bf16[256,16]{0,1:T(8,128)(2,1)S(1)}, f32[256,16]{0,1:T(8,128)}) fusion(s32[256]{0:T(256)S(1)} %copy-done.2, f32[16]{0:T(128)S(1)} %copy-done.3, bf16[16384,16]{1,0:T(8,128)(2,1)} %reshape.33, bf16[256,512]{1,0:T(8,128)(2,1)S(1)} %copy-done.1, bf16[16384,512]{1,0:T(8,128)(2,1)} %all-gather.5.cloned.1.call-done), kind=kOutput, calls=%fused_computation.13 | convolution fusion | flops 4450189312 | bytes 17589312 | tf_op jit(solution)/shard_map/dot_general | solution.py:38
  153.7 0.1 copy.10
  153.9 18.6 %all_gather.19 = bf16[512,128]{1,0:T(8,128)(2,1)S(1)} all-gather(bf16[32,128]{1,0:T(8,128)(2,1)S(1)} %reshape.34), channel_id=1, replica_groups=mesh['groups'=2,'pts'=16] {'pts'}, dimensions={0}, use_global_device_ids=true | all-gather | bytes 139264 | tf_op jit(solution)/shard_map/all_gather | solution.py:44
  172.6 0.7 reshape.35
  173.2 20.2 %all-gather.3.cloned.1.call-done = bf16[4096,512]{1,0:T(8,128)(2,1)} async-done(((bf16[256,512]{1,0:T(8,128)(2,1)}), bf16[4096,512]{1,0:T(8,128)(2,1)}) %all-gather.3.cloned.1.call-update) | async-done | bytes 4194320 | tf_op jit(solution)/shard_map/all_gather | solution.py:43
  193.5 12.9 %fusion.10 = bf16[1024,16]{1,0:T(8,128)(2,1)S(1)} fusion(bf16[4096,16]{1,0:T(8,128)(2,1)S(1)} %reshape.35, bf16[4096,512]{1,0:T(8,128)(2,1)} %all-gather.3.cloned.1.call-done, bf16[1024,512]{1,0:T(8,128)(2,1)S(1)} %copy-done), kind=kOutput, calls=%fused_computation.10 | convolution fusion | flops 4450189312 | bytes 5406720 | tf_op jit(solution)/shard_map/dot_general | solution.py:48
  206.4 13.1 %convolution_bitcast_fusion = f32[16384,16]{0,1:T(8,128)S(1)} fusion(bf16[1024,16]{1,0:T(8,128)(2,1)S(1)} %fusion.10, bf16[1024,16384]{1,0:T(8,128)(2,1)} %param.9), kind=kOutput, calls=%fused_computation.5 | convolution fusion | flops 536870912 | bytes 34635776 | tf_op jit(solution)/shard_map/dot_general | solution.py:56
  219.4 4.6 %copy.11 = f32[16384,16]{1,0:T(8,128)} copy(f32[16384,16]{0,1:T(8,128)S(1)} %convolution_bitcast_fusion) | data formatting | bytes 2097152 | tf_op jit(solution)/shard_map/dot_general | solution.py:56
  224.0 6.5 %reshape.36 = f32[2048,128]{1,0:T(8,128)} reshape(f32[16384,16]{1,0:T(8,128)} %copy.11) | data formatting | bytes 2097152 | tf_op jit(solution)/shard_map/reshape | solution.py:60
  230.5 56.4 %reduce-scatter.2.cloned.1.call-done = f32[128,128]{1,0:T(8,128)} async-done(((f32[2048,128]{1,0:T(8,128)}), f32[128,128]{1,0:T(8,128)}) %reduce-scatter.2.cloned.1.call-update) | async-done | bytes 65552 | tf_op jit(solution)/shard_map/reduce_scatter | solution.py:59
  286.9 1.0 reshape.37
  288.0 0.8 copy.12
  (13 shorter events, 0.3 us)
Async XLA Ops:
  7.2 134.8 %all-gather.5.cloned.1.call-start = ((), (), s32[]{:S(2)}) async-start(), calls=%async_computation.2 | async-start | bytes 17825792 | tf_op jit(solution)/shard_map/all_gather | solution.py:33
  7.9 185.6 %all-gather.3.cloned.1.call-start = ((), (), s32[]{:S(2)}) async-start(), calls=%async_computation.1 | async-start | bytes 4456448 | tf_op jit(solution)/shard_map/all_gather | solution.py:43
  8.6 278.3 %reduce-scatter.2.cloned.1.call-start = ((), (), s32[]{:S(2)}) async-start(), calls=%async_computation.3 | async-start | bytes 1114112 | tf_op jit(solution)/shard_map/reduce_scatter | solution.py:59
  40.3 101.7 %copy-start.1 = (bf16[256,512]{1,0:T(8,128)(2,1)S(1)}, bf16[256,512]{1,0:T(8,128)(2,1)}, u32[]{:S(2)}) copy-start(bf16[256,512]{1,0:T(8,128)(2,1)} %param.6) | copy-start | bytes 786436
  40.3 101.7 %copy-start.2 = (s32[256]{0:T(256)S(1)}, s32[256]{0:T(256)}, u32[]{:S(2)}) copy-start(s32[256]{0:T(256)} %param.7) | copy-start | bytes 3076
  40.3 101.7 %copy-start.3 = (f32[16]{0:T(128)S(1)}, f32[16]{0:T(128)}, u32[]{:S(2)}) copy-start(f32[16]{0:T(128)} %param.11) | copy-start | bytes 196
  80.5 112.9 %copy-start = (bf16[1024,512]{1,0:T(8,128)(2,1)S(1)}, bf16[1024,512]{1,0:T(8,128)(2,1)}, u32[]{:S(2)}) copy-start(bf16[1024,512]{1,0:T(8,128)(2,1)} %param.8) | copy-start | bytes 3145732
Sparse Core Ops, SparseCore 0:
  10.1 131.8 all-gather.4
  144.2 49.2 all-gather.2
  230.6 56.2 reduce-scatter.1
where the time goes:
time: 296 us; the launch traced here: 295 us
  waiting for transfers between devices  140 us (47%)
  blocking collectives  65.5 us (22%)
  matrix products  53.1 us (18%)
  local copies, waits for them, and re-layouts  23.3 us (8%)
  between operations  13.8 us (5%)
    all_gather x1, waiting for transfers between devices, on_device(): lax.all_gather(centres, 'pts', axis=0, tiled=True)  61.5 us
    reduce_scatter x1, waiting for transfers between devices, on_device(): lax.psum_scatter(term.reshape(lax.axis_size('pts') * dense_centres, 128),...  56.4 us
    all_gather x1, blocking collectives, on_device(): beta_part = lax.all_gather(beta_dense, 'pts', axis=0, tiled=True)  26.4 us
    all_gather x1, blocking collectives, on_device(): lax.all_gather(alpha_dense, 'pts', axis=0, tiled=True)  20.5 us
    all_gather x1, waiting for transfers between devices, on_device(): lax.all_gather(points, 'pts', axis=0, tiled=True)  20.2 us
    all_gather x1, blocking collectives, on_device(): lax.all_gather(resid_dense, 'pts', axis=0, tiled=True)  18.6 us
    dot_general x1, matrix products, on_device(): alpha_sum = jnp.dot(columns, narrow, preferred_element_type=jnp.float32)  15.4 us
    dot_general x1, matrix products, on_device(): lax.dot_general(columns, grad_kernel, (((0,), (0,)), ((), ())), preferred...  13.1 us
  transfers between devices with their start and end apart: 3, of which 3 were waited for; matrix products, arithmetic and copies ran while one was open for 13% of the time, Pallas kernels for 0%

commit v1 on v0

--- a/solution.py
+++ b/solution.py
@@ -1,8 +1,27 @@
+import functools
 import math
 import jax
 import jax.numpy as jnp
 from jax import lax
 from jax.sharding import PartitionSpec as P
+from jax.lax import axis_index, axis_size, ppermute
+
+
+def list_paths(original, mesh_ax):
+    many = axis_size(mesh_ax)
+    log = [(j0, (j0 + 1) % many) for j0 in range(many)]
+    gallery = [(j0, (j0 - 1) % many) for j0 in range(many)]
+    right_arr, known = ([original], [original])
+    for _ in range(many // 2):
+        right_arr.append(ppermute(right_arr[-1], axis_name=mesh_ax, perm=log))
+    for _ in range((many - 1) // 2):
+        known.append(ppermute(known[-1], mesh_ax, gallery))
+    taken_in = jnp.concatenate([*right_arr[::-1], *known[1:]], axis=0)
+    o_now = jnp.roll(taken_in, shift=(axis_index(mesh_ax) - many // 2) * original.shape[0], axis=0)
+    return o_now
+
+
+supply_all_shapes_for = functools.partial(list_paths, mesh_ax="pts")
 
 
 def cube_kernel(point_block, centre_block):
@@ -40,7 +59,7 @@
     resid = (jax.nn.sigmoid(logits) - onehot).astype(jnp.bfloat16)
     resid_dense = resid.reshape(local_points // packing, 128)
     parts_in = (
-        lax.all_gather(points, "pts", axis=0, tiled=True),
+        supply_all_shapes_for(points),
         lax.all_gather(resid_dense, "pts", axis=0, tiled=True),
     )
     kernel_tile = cube_kernel(parts_in[0], centres)

time: 296 us -> 328 us (1.11)
  waiting for transfers between devices: 140 us -> 103 us
  local copies, waits for them, and re-layouts: 23.3 us -> 53.1 us
  starting transfers between devices: 0.11 us -> 27.6 us
  blocking collectives: 65.5 us -> 76.6 us
    all_gather x1, waiting for transfers between devices: 61.5 us -> 0.01 us  [on_device(): lax.all_gather(centres, 'pts', axis=0, tiled=True)]
    ppermute x0 -> x15, waiting for transfers between devices: none -> 47.2 us  [the longest x8 30.5 us: list_paths(): right_arr.append(ppermute(right_arr[-1], axis_name=mesh_ax, perm=log))]
    unnamed x10 -> x45, local copies, waits for them, and re-layouts: 1.74 us -> 30.7 us
    ppermute x0 -> x15, starting transfers between devices: none -> 27.5 us  [the longest x7 27 us: list_paths(): known.append(ppermute(known[-1], mesh_ax, gallery))]
    all_gather x1 -> x0, waiting for transfers between devices: 20.2 us -> none  [on_device(): lax.all_gather(points, 'pts', axis=0, tiled=True)]
    all_gather x1, blocking collectives: 26.4 us -> 32.9 us  [on_device(): beta_part = lax.all_gather(beta_dense, 'pts', axis=0, tiled=True)]
  transfers between devices with their start and end apart: 3 -> 17, of which waited for: 3 -> 10; matrix products, arithmetic and copies ran while one was open for 13% -> 17% of each run, Pallas kernels for 0% -> 0%
where the time goes in v1:
time: 328 us
  waiting for transfers between devices  103 us (31%)
  blocking collectives  76.6 us (23%)
  local copies, waits for them, and re-layouts  53.1 us (16%)
  matrix products  53 us (16%)
  starting transfers between devices  27.6 us (8%)
  between operations  14.2 us (4%)
    reduce_scatter x1, waiting for transfers between devices, on_device(): lax.psum_scatter(term.reshape(lax.axis_size('pts') * dense_centres, 128),...  55.2 us
    all_gather x1, blocking collectives, on_device(): beta_part = lax.all_gather(beta_dense, 'pts', axis=0, tiled=True)  32.9 us
    unnamed x45, local copies, waits for them, and re-layouts  30.7 us
    ppermute x8, waiting for transfers between devices, list_paths(): right_arr.append(ppermute(right_arr[-1], axis_name=mesh_ax, perm=log))  30.5 us
    ppermute x7, starting transfers between devices, list_paths(): known.append(ppermute(known[-1], mesh_ax, gallery))  27 us
    all_gather x1, blocking collectives, on_device(): lax.all_gather(alpha_dense, 'pts', axis=0, tiled=True)  23.3 us
    all_gather x1, blocking collectives, on_device(): lax.all_gather(resid_dense, 'pts', axis=0, tiled=True)  20.3 us
    ppermute x7, waiting for transfers between devices, list_paths(): known.append(ppermute(known[-1], mesh_ax, gallery))  16.7 us
  transfers between devices with their start and end apart: 17, of which 10 were waited for; matrix products, arithmetic and copies ran while one was open for 17% of the time, Pallas kernels for 0%

profile of v1, /device:TPU:0, one launch (start us, length us, event | category | flops | bytes accessed | tf_op | source)
XLA Modules:
  0.0 327.6 jit_solution(6182492206873567492)
XLA Ops:
  8.5 9.2 %collective-permute-done = bf16[256,512]{1,0:T(8,128)(2,1)S(1)} collective-permute-done((bf16[256,512]{1,0:T(8,128)(2,1)}, bf16[256,512]{1,0:T(8,128)(2,1)S(1)}, u32[]{:S(2)}, u32[]{:S(2)}) %collective-permute-start) | collective-permute-done | bytes 262176 | tf_op jit(solution)/shard_map/ppermute | solution.py:16
  17.7 4.4 %collective-permute-start.8 = (bf16[256,512]{1,0:T(8,128)(2,1)}, bf16[256,512]{1,0:T(8,128)(2,1)S(1)}, u32[]{:S(2)}, u32[]{:S(2)}) collective-permute-start(bf16[256,512]{1,0:T(8,128)(2,1)} %param.6), channel_id=1, source_target_pairs={{0,15},{1,0},{2,1},{3,2},{4,3},{5,4},{6,5},{7,6},{8,7},{9,8},{10,9... | collective-permute-start | bytes 786440 | tf_op jit(solution)/shard_map/ppermute | solution.py:18
  22.2 4.1 %collective-permute-done.1 = bf16[256,512]{1,0:T(8,128)(2,1)S(1)} collective-permute-done((bf16[256,512]{1,0:T(8,128)(2,1)S(1)}, bf16[256,512]{1,0:T(8,128)(2,1)S(1)}, u32[]{:S(2)}, u32[]{:S(2)}) %collective-permute-start.1) | collective-permute-done | bytes 262176 | tf_op jit(solution)/shard_map/ppermute | solution.py:16
  26.3 5.6 %collective-permute-done.8 = bf16[256,512]{1,0:T(8,128)(2,1)S(1)} collective-permute-done((bf16[256,512]{1,0:T(8,128)(2,1)}, bf16[256,512]{1,0:T(8,128)(2,1)S(1)}, u32[]{:S(2)}, u32[]{:S(2)}) %collective-permute-start.8) | collective-permute-done | bytes 262176 | tf_op jit(solution)/shard_map/ppermute | solution.py:18
  32.0 4.5 %collective-permute-start.9 = (bf16[256,512]{1,0:T(8,128)(2,1)S(1)}, bf16[256,512]{1,0:T(8,128)(2,1)S(1)}, u32[]{:S(2)}, u32[]{:S(2)}) collective-permute-start(bf16[256,512]{1,0:T(8,128)(2,1)S(1)} %collective-permute-done.8), channel_id=1, source_target_pairs={{0,15},{1,0},{2,1},{3,2},{4,3},{5,4},{6,5},{7,6},{8,7},{9,8},{10,9... | collective-permute-start | bytes 786440 | tf_op jit(solution)/shard_map/ppermute | solution.py:18
  36.5 4.1 %collective-permute-done.2 = bf16[256,512]{1,0:T(8,128)(2,1)S(1)} collective-permute-done((bf16[256,512]{1,0:T(8,128)(2,1)S(1)}, bf16[256,512]{1,0:T(8,128)(2,1)S(1)}, u32[]{:S(2)}, u32[]{:S(2)}) %collective-permute-start.2) | collective-permute-done | bytes 262176 | tf_op jit(solution)/shard_map/ppermute | solution.py:16
  40.6 5.5 %collective-permute-done.9 = bf16[256,512]{1,0:T(8,128)(2,1)S(1)} collective-permute-done((bf16[256,512]{1,0:T(8,128)(2,1)S(1)}, bf16[256,512]{1,0:T(8,128)(2,1)S(1)}, u32[]{:S(2)}, u32[]{:S(2)}) %collective-permute-start.9) | collective-permute-done | bytes 262176 | tf_op jit(solution)/shard_map/ppermute | solution.py:18
  46.1 4.6 %collective-permute-start.10 = (bf16[256,512]{1,0:T(8,128)(2,1)S(1)}, bf16[256,512]{1,0:T(8,128)(2,1)S(1)}, u32[]{:S(2)}, u32[]{:S(2)}) collective-permute-start(bf16[256,512]{1,0:T(8,128)(2,1)S(1)} %collective-permute-done.9), channel_id=1, source_target_pairs={{0,15},{1,0},{2,1},{3,2},{4,3},{5,4},{6,5},{7,6},{8,7},{9,8},{10,9... | collective-permute-start | bytes 786440 | tf_op jit(solution)/shard_map/ppermute | solution.py:18
  54.8 5.5 %collective-permute-done.10 = bf16[256,512]{1,0:T(8,128)(2,1)S(1)} collective-permute-done((bf16[256,512]{1,0:T(8,128)(2,1)S(1)}, bf16[256,512]{1,0:T(8,128)(2,1)S(1)}, u32[]{:S(2)}, u32[]{:S(2)}) %collective-permute-start.10) | collective-permute-done | bytes 262176 | tf_op jit(solution)/shard_map/ppermute | solution.py:18
  60.4 4.6 %collective-permute-start.11 = (bf16[256,512]{1,0:T(8,128)(2,1)S(1)}, bf16[256,512]{1,0:T(8,128)(2,1)S(1)}, u32[]{:S(2)}, u32[]{:S(2)}) collective-permute-start(bf16[256,512]{1,0:T(8,128)(2,1)S(1)} %collective-permute-done.10), channel_id=1, source_target_pairs={{0,15},{1,0},{2,1},{3,2},{4,3},{5,4},{6,5},{7,6},{8,7},{9,8},{10,9... | collective-permute-start | bytes 786440 | tf_op jit(solution)/shard_map/ppermute | solution.py:18
  65.0 4.1 %collective-permute-done.4 = bf16[256,512]{1,0:T(8,128)(2,1)S(1)} collective-permute-done((bf16[256,512]{1,0:T(8,128)(2,1)S(1)}, bf16[256,512]{1,0:T(8,128)(2,1)S(1)}, u32[]{:S(2)}, u32[]{:S(2)}) %collective-permute-start.4) | collective-permute-done | bytes 262176 | tf_op jit(solution)/shard_map/ppermute | solution.py:16
  69.1 4.5 %collective-permute-start.12 = (bf16[256,512]{1,0:T(8,128)(2,1)S(1)}, bf16[256,512]{1,0:T(8,128)(2,1)S(1)}, u32[]{:S(2)}, u32[]{:S(2)}) collective-permute-start(bf16[256,512]{1,0:T(8,128)(2,1)S(1)} %collective-permute-done.11), channel_id=1, source_target_pairs={{0,15},{1,0},{2,1},{3,2},{4,3},{5,4},{6,5},{7,6},{8,7},{9,8},{10,9... | collective-permute-start | bytes 786440 | tf_op jit(solution)/shard_map/ppermute | solution.py:18
  73.6 4.8 %collective-permute-done.5 = bf16[256,512]{1,0:T(8,128)(2,1)S(1)} collective-permute-done((bf16[256,512]{1,0:T(8,128)(2,1)S(1)}, bf16[256,512]{1,0:T(8,128)(2,1)S(1)}, u32[]{:S(2)}, u32[]{:S(2)}) %collective-permute-start.5) | collective-permute-done | bytes 262176 | tf_op jit(solution)/shard_map/ppermute | solution.py:16
  79.5 32.9 %all_gather.13 = bf16[2048,128]{1,0:T(8,128)(2,1)S(1)} all-gather(bf16[128,128]{1,0:T(8,128)(2,1)S(1)} %reshape.30), channel_id=1, replica_groups=mesh['groups'=2,'pts'=16] {'pts'}, dimensions={0}, use_global_device_ids=true | all-gather | bytes 557056 | tf_op jit(solution)/shard_map/all_gather | solution.py:43
  116.4 4.3 %collective-permute-start.13 = (bf16[256,512]{1,0:T(8,128)(2,1)S(1)}, bf16[256,512]{1,0:T(8,128)(2,1)}, u32[]{:S(2)}, u32[]{:S(2)}) collective-permute-start(bf16[256,512]{1,0:T(8,128)(2,1)S(1)} %collective-permute-done.12), channel_id=1, source_target_pairs={{0,15},{1,0},{2,1},{3,2},{4,3},{5,4},{6,5},{7,6},{8,7},{9,8},{10,9... | collective-permute-start | bytes 786440 | tf_op jit(solution)/shard_map/ppermute | solution.py:18
  120.7 15.3 %convolution_convert_fusion = bf16[1024,16]{0,1:T(8,128)(2,1)S(1)} fusion(bf16[1024,16384]{1,0:T(8,128)(2,1)} %param.9, bf16[16384,16]{1,0:T(8,128)(2,1)} %reshape.31), kind=kOutput, calls=%fused_computation.12 | convolution fusion | flops 536887296 | bytes 34111488 | tf_op jit(solution)/shard_map/dot_general | solution.py:46
  136.3 23.3 %all_gather.14 = bf16[2048,128]{1,0:T(8,128)(2,1)S(1)} all-gather(bf16[128,128]{1,0:T(8,128)(2,1)S(1)} %reshape.32), channel_id=1, replica_groups=mesh['groups'=2,'pts'=16] {'pts'}, dimensions={0}, use_global_device_ids=true | all-gather | bytes 557056 | tf_op jit(solution)/shard_map/all_gather | solution.py:53
  193.6 11.8 %subtract_convert_fusion = (bf16[256,16]{0,1:T(8,128)(2,1)S(1)}, f32[256,16]{0,1:T(8,128)}) fusion(s32[256]{0:T(256)S(1)} %copy-done.4, f32[16]{0:T(128)S(1)} %copy-done.5, bf16[16384,16]{1,0:T(8,128)(2,1)} %reshape.33, bf16[256,512]{1,0:T(8,128)(2,1)S(1)} %copy-done.1, bf16[16384,512]{1,0:T(8,128)(2,1)} %all-gather.2.cloned.1.call-done), kind=kOutput, calls=%fused_computation.46 | convolution fusion | flops 4450189312 | bytes 17589312 | tf_op jit(solution)/shard_map/dot_general | solution.py:57
  205.6 20.3 %all_gather.15 = bf16[512,128]{1,0:T(8,128)(2,1)S(1)} all-gather(bf16[32,128]{1,0:T(8,128)(2,1)S(1)} %reshape.34), channel_id=1, replica_groups=mesh['groups'=2,'pts'=16] {'pts'}, dimensions={0}, use_global_device_ids=true | all-gather | bytes 139264 | tf_op jit(solution)/shard_map/all_gather | solution.py:63
  226.6 12.9 %fusion.14 = bf16[1024,16]{1,0:T(8,128)(2,1)S(1)} fusion(bf16[4096,16]{1,0:T(8,128)(2,1)S(1)} %reshape.35, bf16[1024,512]{1,0:T(8,128)(2,1)S(1)} %copy-done, bf16[8192,512]{1,0:T(8,128)(2,1)} %constant_dynamic-update-slice_fusion, s32[]{:T(128)S(6)} %select_n.14), kind=kOutput, calls=%fused_computation.11 | convolution fusion | flops 4450189312 | bytes 5406724 | tf_op jit(solution)/shard_map/dot_general | solution.py:67
  239.5 13.1 %convolution_bitcast_fusion = f32[16384,16]{0,1:T(8,128)S(1)} fusion(bf16[1024,16]{1,0:T(8,128)(2,1)S(1)} %fusion.14, bf16[1024,16384]{1,0:T(8,128)(2,1)} %param.9), kind=kOutput, calls=%fused_computation.5 | convolution fusion | flops 536870912 | bytes 34635776 | tf_op jit(solution)/shard_map/dot_general | solution.py:75
  252.6 4.6 %copy.11 = f32[16384,16]{1,0:T(8,128)} copy(f32[16384,16]{0,1:T(8,128)S(1)} %convolution_bitcast_fusion) | data formatting | bytes 2097152 | tf_op jit(solution)/shard_map/dot_general | solution.py:75
  257.2 6.5 %reshape.36 = f32[2048,128]{1,0:T(8,128)} reshape(f32[16384,16]{1,0:T(8,128)} %copy.11) | data formatting | bytes 2097152 | tf_op jit(solution)/shard_map/reshape | solution.py:79
  263.7 55.2 %reduce-scatter.2.cloned.1.call-done = f32[128,128]{1,0:T(8,128)} async-done(((f32[2048,128]{1,0:T(8,128)}), f32[128,128]{1,0:T(8,128)}) %reduce-scatter.2.cloned.1.call-update) | async-done | bytes 65552 | tf_op jit(solution)/shard_map/reduce_scatter | solution.py:78
  (76 shorter events, 47.5 us)
Async XLA Ops:
  7.2 186.4 %all-gather.2.cloned.1.call-start = ((), (), s32[]{:S(2)}) async-start(), calls=%async_computation.1 | async-start | bytes 17825792 | tf_op jit(solution)/shard_map/all_gather | solution.py:52
  7.9 311.0 %reduce-scatter.2.cloned.1.call-start = ((), (), s32[]{:S(2)}) async-start(), calls=%async_computation.2 | async-start | bytes 1114112 | tf_op jit(solution)/shard_map/reduce_scatter | solution.py:78
  7.9 9.8 %collective-permute-start = (bf16[256,512]{1,0:T(8,128)(2,1)}, bf16[256,512]{1,0:T(8,128)(2,1)S(1)}, u32[]{:S(2)}, u32[]{:S(2)}) collective-permute-start(bf16[256,512]{1,0:T(8,128)(2,1)} %param.6), channel_id=1, source_target_pairs={{0,1},{1,2},{2,3},{3,4},{4,5},{5,6},{6,7},{7,8},{8,9},{9,10},{10,1... | collective-permute-start | bytes 786440 | tf_op jit(solution)/shard_map/ppermute | solution.py:16
  17.7 8.6 %collective-permute-start.1 = (bf16[256,512]{1,0:T(8,128)(2,1)S(1)}, bf16[256,512]{1,0:T(8,128)(2,1)S(1)}, u32[]{:S(2)}, u32[]{:S(2)}) collective-permute-start(bf16[256,512]{1,0:T(8,128)(2,1)S(1)} %collective-permute-done), channel_id=1, source_target_pairs={{0,1},{1,2},{2,3},{3,4},{4,5},{5,6},{6,7},{7,8},{8,9},{9,10},{10,1... | collective-permute-start | bytes 786440 | tf_op jit(solution)/shard_map/ppermute | solution.py:16
  17.7 14.2 %collective-permute-start.8 = (bf16[256,512]{1,0:T(8,128)(2,1)}, bf16[256,512]{1,0:T(8,128)(2,1)S(1)}, u32[]{:S(2)}, u32[]{:S(2)}) collective-permute-start(bf16[256,512]{1,0:T(8,128)(2,1)} %param.6), channel_id=1, source_target_pairs={{0,15},{1,0},{2,1},{3,2},{4,3},{5,4},{6,5},{7,6},{8,7},{9,8},{10,9... | collective-permute-start | bytes 786440 | tf_op jit(solution)/shard_map/ppermute | solution.py:18
  26.3 14.2 %collective-permute-start.2 = (bf16[256,512]{1,0:T(8,128)(2,1)S(1)}, bf16[256,512]{1,0:T(8,128)(2,1)S(1)}, u32[]{:S(2)}, u32[]{:S(2)}) collective-permute-start(bf16[256,512]{1,0:T(8,128)(2,1)S(1)} %collective-permute-done.1), channel_id=1, source_target_pairs={{0,1},{1,2},{2,3},{3,4},{4,5},{5,6},{6,7},{7,8},{8,9},{9,10},{10,1... | collective-permute-start | bytes 786440 | tf_op jit(solution)/shard_map/ppermute | solution.py:16
  32.0 14.2 %collective-permute-start.9 = (bf16[256,512]{1,0:T(8,128)(2,1)S(1)}, bf16[256,512]{1,0:T(8,128)(2,1)S(1)}, u32[]{:S(2)}, u32[]{:S(2)}) collective-permute-start(bf16[256,512]{1,0:T(8,128)(2,1)S(1)} %collective-permute-done.8), channel_id=1, source_target_pairs={{0,15},{1,0},{2,1},{3,2},{4,3},{5,4},{6,5},{7,6},{8,7},{9,8},{10,9... | collective-permute-start | bytes 786440 | tf_op jit(solution)/shard_map/ppermute | solution.py:18
  40.6 14.2 %collective-permute-start.3 = (bf16[256,512]{1,0:T(8,128)(2,1)S(1)}, bf16[256,512]{1,0:T(8,128)(2,1)S(1)}, u32[]{:S(2)}, u32[]{:S(2)}) collective-permute-start(bf16[256,512]{1,0:T(8,128)(2,1)S(1)} %collective-permute-done.2), channel_id=1, source_target_pairs={{0,1},{1,2},{2,3},{3,4},{4,5},{5,6},{6,7},{7,8},{8,9},{9,10},{10,1... | collective-permute-start | bytes 786440 | tf_op jit(solution)/shard_map/ppermute | solution.py:16
  46.1 14.2 %collective-permute-start.10 = (bf16[256,512]{1,0:T(8,128)(2,1)S(1)}, bf16[256,512]{1,0:T(8,128)(2,1)S(1)}, u32[]{:S(2)}, u32[]{:S(2)}) collective-permute-start(bf16[256,512]{1,0:T(8,128)(2,1)S(1)} %collective-permute-done.9), channel_id=1, source_target_pairs={{0,15},{1,0},{2,1},{3,2},{4,3},{5,4},{6,5},{7,6},{8,7},{9,8},{10,9... | collective-permute-start | bytes 786440 | tf_op jit(solution)/shard_map/ppermute | solution.py:18
  54.8 14.2 %collective-permute-start.4 = (bf16[256,512]{1,0:T(8,128)(2,1)S(1)}, bf16[256,512]{1,0:T(8,128)(2,1)S(1)}, u32[]{:S(2)}, u32[]{:S(2)}) collective-permute-start(bf16[256,512]{1,0:T(8,128)(2,1)S(1)} %collective-permute-done.3), channel_id=1, source_target_pairs={{0,1},{1,2},{2,3},{3,4},{4,5},{5,6},{6,7},{7,8},{8,9},{9,10},{10,1... | collective-permute-start | bytes 786440 | tf_op jit(solution)/shard_map/ppermute | solution.py:16
  60.4 8.7 %collective-permute-start.11 = (bf16[256,512]{1,0:T(8,128)(2,1)S(1)}, bf16[256,512]{1,0:T(8,128)(2,1)S(1)}, u32[]{:S(2)}, u32[]{:S(2)}) collective-permute-start(bf16[256,512]{1,0:T(8,128)(2,1)S(1)} %collective-permute-done.10), channel_id=1, source_target_pairs={{0,15},{1,0},{2,1},{3,2},{4,3},{5,4},{6,5},{7,6},{8,7},{9,8},{10,9... | collective-permute-start | bytes 786440 | tf_op jit(solution)/shard_map/ppermute | solution.py:18
  69.1 9.3 %collective-permute-start.5 = (bf16[256,512]{1,0:T(8,128)(2,1)S(1)}, bf16[256,512]{1,0:T(8,128)(2,1)S(1)}, u32[]{:S(2)}, u32[]{:S(2)}) collective-permute-start(bf16[256,512]{1,0:T(8,128)(2,1)S(1)} %collective-permute-done.4), channel_id=1, source_target_pairs={{0,1},{1,2},{2,3},{3,4},{4,5},{5,6},{6,7},{7,8},{8,9},{9,10},{10,1... | collective-permute-start | bytes 786440 | tf_op jit(solution)/shard_map/ppermute | solution.py:16
  69.1 47.3 %collective-permute-start.12 = (bf16[256,512]{1,0:T(8,128)(2,1)S(1)}, bf16[256,512]{1,0:T(8,128)(2,1)S(1)}, u32[]{:S(2)}, u32[]{:S(2)}) collective-permute-start(bf16[256,512]{1,0:T(8,128)(2,1)S(1)} %collective-permute-done.11), channel_id=1, source_target_pairs={{0,15},{1,0},{2,1},{3,2},{4,3},{5,4},{6,5},{7,6},{8,7},{9,8},{10,9... | collective-permute-start | bytes 786440 | tf_op jit(solution)/shard_map/ppermute | solution.py:18
  78.4 42.3 %copy-start.2 = (bf16[256,512]{1,0:T(8,128)(2,1)}, bf16[256,512]{1,0:T(8,128)(2,1)S(1)}, u32[]{:S(2)}) copy-start(bf16[256,512]{1,0:T(8,128)(2,1)S(1)} %collective-permute-done.5) | copy-start | bytes 786436
  78.4 42.3 %collective-permute-start.6 = (bf16[256,512]{1,0:T(8,128)(2,1)S(1)}, bf16[256,512]{1,0:T(8,128)(2,1)}, u32[]{:S(2)}, u32[]{:S(2)}) collective-permute-start(bf16[256,512]{1,0:T(8,128)(2,1)S(1)} %collective-permute-done.5), channel_id=1, source_target_pairs={{0,1},{1,2},{2,3},{3,4},{4,5},{5,6},{6,7},{7,8},{8,9},{9,10},{10,1... | collective-permute-start | bytes 786440 | tf_op jit(solution)/shard_map/ppermute | solution.py:16
  116.4 47.3 %collective-permute-start.13 = (bf16[256,512]{1,0:T(8,128)(2,1)S(1)}, bf16[256,512]{1,0:T(8,128)(2,1)}, u32[]{:S(2)}, u32[]{:S(2)}) collective-permute-start(bf16[256,512]{1,0:T(8,128)(2,1)S(1)} %collective-permute-done.12), channel_id=1, source_target_pairs={{0,15},{1,0},{2,1},{3,2},{4,3},{5,4},{6,5},{7,6},{8,7},{9,8},{10,9... | collective-permute-start | bytes 786440 | tf_op jit(solution)/shard_map/ppermute | solution.py:18
  120.7 43.1 %collective-permute-start.7 = (bf16[256,512]{1,0:T(8,128)(2,1)}, bf16[256,512]{1,0:T(8,128)(2,1)}, u32[]{:S(2)}, u32[]{:S(2)}) collective-permute-start(bf16[256,512]{1,0:T(8,128)(2,1)} %collective-permute-done.6), channel_id=1, source_target_pairs={{0,1},{1,2},{2,3},{3,4},{4,5},{5,6},{6,7},{7,8},{8,9},{9,10},{10,1... | collective-permute-start | bytes 786440 | tf_op jit(solution)/shard_map/ppermute | solution.py:16
  135.9 36.5 %copy-start.1 = (bf16[256,512]{1,0:T(8,128)(2,1)S(1)}, bf16[256,512]{1,0:T(8,128)(2,1)}, u32[]{:S(2)}) copy-start(bf16[256,512]{1,0:T(8,128)(2,1)} %param.6) | copy-start | bytes 786436
  163.7 18.8 %copy-start.3 = (bf16[256,512]{1,0:T(8,128)(2,1)S(1)}, bf16[256,512]{1,0:T(8,128)(2,1)}, u32[]{:S(2)}) copy-start(bf16[256,512]{1,0:T(8,128)(2,1)} %copy-done.2) | copy-start | bytes 786436
  163.7 29.9 %copy-start.4 = (s32[256]{0:T(256)S(1)}, s32[256]{0:T(256)}, u32[]{:S(2)}) copy-start(s32[256]{0:T(256)} %param.7) | copy-start | bytes 3076
  163.7 29.9 %copy-start.5 = (f32[16]{0:T(128)S(1)}, f32[16]{0:T(128)}, u32[]{:S(2)}) copy-start(f32[16]{0:T(128)} %param.11) | copy-start | bytes 196
  163.7 14.7 %collective-permute-start.14 = (bf16[256,512]{1,0:T(8,128)(2,1)}, bf16[256,512]{1,0:T(8,128)(2,1)S(1)}, u32[]{:S(2)}, u32[]{:S(2)}) collective-permute-start(bf16[256,512]{1,0:T(8,128)(2,1)} %collective-permute-done.13), channel_id=1, source_target_pairs={{0,15},{1,0},{2,1},{3,2},{4,3},{5,4},{6,5},{7,6},{8,7},{9,8},{10,9... | collective-permute-start | bytes 786440 | tf_op jit(solution)/shard_map/ppermute | solution.py:18
  193.5 33.0 %copy-start = (bf16[1024,512]{1,0:T(8,128)(2,1)S(1)}, bf16[1024,512]{1,0:T(8,128)(2,1)}, u32[]{:S(2)}) copy-start(bf16[1024,512]{1,0:T(8,128)(2,1)} %param.8) | copy-start | bytes 3145732
Sparse Core Ops, SparseCore 0:
  10.1 154.9 all-gather.1
  263.8 55.0 reduce-scatter.1
